TPU v7x, 32 devices: a whole 2x2x4 slice. The times are simulated.
32 devices in a mesh: dp: 4 (over y, core), row: 4 (over z), col: 2 (over x).
Axes of the slice: x: 2, y: 2, z: 4, core: 2. Of those that a mesh axis runs over, the one named last changes fastest.
Arguments:
- inputs: bfloat16 [4096, 1024], P(('dp', 'col'), 'row'), may hold values from -6 to 6
- cotangent: bfloat16 [4096, 1024], P(('dp', 'col'), 'row'), may hold values from -6 to 6
- seg_parent: int32 [52], P('dp'), may hold values from 0 to 51, as said below
- token_depth: int32 [4096], P('dp'), may hold values from 0 to 383, as said below
- ln1_gain: float32 [1024], P('row'), may hold values from 0.25 to 1.75
- ln1_bias: float32 [1024], P('row'), may hold values from -1.5 to 1.5
- w_qkv: bfloat16 [1024, 3, 1024], P('row', None, 'col'), may hold values from -0.1875 to 0.1875
- b_qv: float32 [2, 1024], P(None, 'col'), may hold values from -1.5 to 1.5
- w_out: bfloat16 [1024, 1024], P('col', 'row'), may hold values from -0.5 to 0.5
- b_out: float32 [1024], P('row'), may hold values from -1.5 to 1.5
- ln2_gain: float32 [1024], P('row'), may hold values from 0.25 to 1.75
- ln2_bias: float32 [1024], P('row'), may hold values from -1.5 to 1.5
- w_up: bfloat16 [1024, 4096], P('row', 'col'), may hold values from -0.1875 to 0.1875
- b_up: float32 [4096], P('col'), may hold values from -1.5 to 1.5
- w_down: bfloat16 [4096, 1024], P('col', 'row'), may hold values from -0.125 to 0.125
- b_down: float32 [1024], P('row'), may hold values from -1.5 to 1.5
Outputs:
- result: float32 [4096, 1024], P(('dp', 'col'), 'row')
- input_grad: float32 [4096, 1024], P(('dp', 'col'), 'row')
- grad_ln1_gain: float32 [1024], P('row')
- grad_ln1_bias: float32 [1024], P('row')
- grad_w_qkv: float32 [1024, 3, 1024], P('row', None, 'col')
- grad_b_qv: float32 [2, 1024], P(None, 'col')
- grad_w_out: float32 [1024, 1024], P('col', 'row')
- grad_b_out: float32 [1024], P('row')
- grad_ln2_gain: float32 [1024], P('row')
- grad_ln2_bias: float32 [1024], P('row')
- grad_w_up: float32 [1024, 4096], P('row', 'col')
- grad_b_up: float32 [4096], P('col')
- grad_w_down: float32 [4096, 1024], P('col', 'row')
- grad_b_down: float32 [1024], P('row')
Inputs may be any that keep to these rules, and one draw needn't show every extreme that they name: `seg_parent`: tree t holds tokens t * 1024 to (t + 1) * 1024 - 1 and segments 13 t to 13 t + 12, laid out as segment(i) says: segment 13 t is the trunk of 256 tokens and is its own parent; four of the other twelve are branches with the trunk as parent, eight are leaves, two for every branch, with that branch as parent; segment 13 t + 12 is a branch; which ids play the other parts is drawn. `token_depth`: the token at offset j of its segment has depth j in a trunk, 256 + j in a branch and 320 + j in a leaf.
All inputs are finite; a program needn't handle non-finite values.
Results may differ from a plain program's by a relative error of at most 0.011.
Values may be sent and summed in bfloat16 or wider, within the bound.
A program may use at most 192 MiB of HBM per device.

v0:
```python
import math
import jax
import jax.numpy as jnp
from jax import lax
from jax.sharding import PartitionSpec as P

HD = 128
EPS = 1e-05
MASKED = -1e30


def gelu_value(values):
    return 0.5 * values * (1.0 + jax.scipy.special.erf(values / math.sqrt(2.0)))


def gelu_slope(values):
    return 0.5 * (1.0 + jax.scipy.special.erf(values / math.sqrt(2.0))) + values * jnp.exp(
        -0.5 * values * values
    ) / math.sqrt(2.0 * math.pi)


def width_sums(first_term, second_term):
    return lax.psum((jnp.sum(first_term, axis=1), jnp.sum(second_term, axis=1)), "row")


def normalize(values, norm_gain, norm_bias, feature_count):
    row_total, square = width_sums(values, values * values)
    row_mean = row_total / feature_count
    inv_std = lax.rsqrt(square / feature_count - row_mean * row_mean + EPS)
    normed = (values - row_mean[:, None]) * inv_std[:, None]
    return (normed, inv_std, (normed * norm_gain + norm_bias).astype(jnp.bfloat16))


def normalize_back(upstream, normed, inv_std, norm_gain, feature_count):
    spread = upstream * norm_gain
    row_total, cross_sum = width_sums(spread, spread * normed)
    return inv_std[:, None] * (
        spread - row_total[:, None] / feature_count - normed * (cross_sum[:, None] / feature_count)
    )


def contract(left_op, right_op, flipped):
    if flipped:
        return lax.dot_general(
            left_op, right_op, (((1,), (1,)), ((), ())), preferred_element_type=jnp.float32
        )
    return jnp.dot(left_op, right_op, preferred_element_type=jnp.float32)


def outer_sum(left_op, right_op):
    return lax.dot_general(
        left_op, right_op, (((0,), (0,)), ((), ())), preferred_element_type=jnp.float32
    )


def across_rows(operand, weight_block, flipped):
    gathered = lax.all_gather(operand, "col", axis=0, tiled=True)
    row_count = gathered.shape[0] // lax.axis_size("row")

    def partial_term(row_start, row_num):
        return contract(gathered, weight_block, flipped)

    return (
        lax.psum_scatter(
            partial_term(jnp.int32(0), row_count * lax.axis_size("row")),
            "row",
            scatter_dimension=0,
            tiled=True,
        ),
        gathered,
    )


def across_cols(operand, weight_block, flipped):
    gathered = lax.all_gather(operand, "row", axis=0, tiled=True)
    row_count = gathered.shape[0] // lax.axis_size("col")

    def partial_term(row_start, row_num):
        return contract(gathered, weight_block, flipped)

    return (
        lax.psum_scatter(
            partial_term(jnp.int32(0), row_count * lax.axis_size("col")),
            "col",
            scatter_dimension=0,
            tiled=True,
        ),
        gathered,
    )


def tree_labels(seg_parent, token_depth):
    seg_count = seg_parent.shape[0]
    tree_len = token_depth.shape[0]
    seg_len = tree_len // 16
    slot_ids = jnp.arange(seg_count, dtype=jnp.int32)
    where_at = jnp.arange(tree_len, dtype=jnp.int32)
    segment = jnp.where(where_at < 4 * seg_len, 0, 1 + (where_at - 4 * seg_len) // seg_len)
    parent_local = seg_parent - lax.axis_index("dp") * seg_count
    parent_one = jnp.sum(
        jnp.where(segment[:, None] == slot_ids[None, :], parent_local[None, :], 0), axis=1
    )
    parent_two = jnp.sum(
        jnp.where(parent_one[:, None] == slot_ids[None, :], parent_local[None, :], 0), axis=1
    )
    return (segment, parent_one, parent_two, token_depth)


def block_scores(query_block, key_rows, labels, query_start, slopes):
    segment, parent_one, parent_two, token_depth = labels
    block_size = query_block.shape[0]
    query_seg = lax.dynamic_slice_in_dim(segment, query_start, block_size, 0)
    query_one = lax.dynamic_slice_in_dim(parent_one, query_start, block_size, 0)
    query_two = lax.dynamic_slice_in_dim(parent_two, query_start, block_size, 0)
    query_depth = lax.dynamic_slice_in_dim(token_depth, query_start, block_size, 0)
    allowed = (
        (segment[None, :] == query_seg[:, None])
        | (segment[None, :] == query_one[:, None])
        | (segment[None, :] == query_two[:, None])
    ) & (token_depth[None, :] <= query_depth[:, None])
    score_scale = query_block.shape[2] ** (-0.5)
    raw = jnp.einsum("qhd,khd->hqk", query_block, key_rows, preferred_element_type=jnp.float32)
    distance = (query_depth[:, None] - token_depth[None, :]).astype(jnp.float32)
    scores = raw * score_scale - slopes[:, None, None] * distance[None]
    return jnp.where(allowed[None], scores, MASKED)


def attention_forward(queries, key_rows, value_rows, labels, slopes, offset):
    block_size = min(512, queries.shape[0])
    blocks = queries.shape[0] // block_size

    def one_block(block_index):
        block_first = block_index * block_size
        query_block = lax.dynamic_slice_in_dim(queries, block_first, block_size, 0)
        scores = block_scores(query_block, key_rows, labels, offset + block_first, slopes)
        top_score = jnp.max(scores, axis=2, keepdims=True)
        weights = jnp.exp(scores - top_score)
        weight_total = jnp.sum(weights, axis=2, keepdims=True)
        probs = (weights / weight_total).astype(jnp.bfloat16)
        mixed = jnp.einsum("hqk,khd->qhd", probs, value_rows, preferred_element_type=jnp.float32)
        return (mixed, (top_score + jnp.log(weight_total))[:, :, 0])

    return lax.map(one_block, jnp.arange(blocks, dtype=jnp.int32))


def attention_backward(
    queries, key_rows, value_rows, grad_mixed, log_total, labels, slopes, offset
):
    block_size = min(512, queries.shape[0])
    blocks = queries.shape[0] // block_size
    score_scale = queries.shape[2] ** (-0.5)

    def one_block(carry, items):
        key_grad, value_grad = carry
        block_index, block_total = items
        block_first = block_index * block_size
        query_block = lax.dynamic_slice_in_dim(queries, block_first, block_size, 0)
        grad_block = lax.dynamic_slice_in_dim(grad_mixed, block_first, block_size, 0)
        scores = block_scores(query_block, key_rows, labels, offset + block_first, slopes)
        probs = jnp.exp(scores - block_total[:, :, None])
        grad_probs = jnp.einsum(
            "qhd,khd->hqk", grad_block, value_rows, preferred_element_type=jnp.float32
        )
        centre = jnp.sum(probs * grad_probs, axis=2, keepdims=True)
        grad_scores = (probs * (grad_probs - centre)).astype(jnp.bfloat16)
        query_grad = (
            jnp.einsum("hqk,khd->qhd", grad_scores, key_rows, preferred_element_type=jnp.float32)
            * score_scale
        )
        key_grad = (
            key_grad
            + jnp.einsum(
                "hqk,qhd->khd", grad_scores, query_block, preferred_element_type=jnp.float32
            )
            * score_scale
        )
        value_grad = value_grad + jnp.einsum(
            "hqk,qhd->khd",
            probs.astype(jnp.bfloat16),
            grad_block,
            preferred_element_type=jnp.float32,
        )
        return ((key_grad, value_grad), query_grad)

    empty = jnp.zeros(key_rows.shape, jnp.float32)
    (key_grad, value_grad), query_grad = lax.scan(
        one_block, (empty, empty), (jnp.arange(blocks, dtype=jnp.int32), log_total)
    )
    return (key_grad, value_grad, query_grad)


def on_device(
    inputs,
    cotangent,
    seg_parent,
    token_depth,
    ln1_gain,
    ln1_bias,
    w_qkv,
    b_qv,
    w_out,
    b_out,
    ln2_gain,
    ln2_bias,
    w_up,
    b_up,
    w_down,
    b_down,
):
    feature_count = inputs.shape[1] * lax.axis_size("row")
    col_width = w_qkv.shape[2]
    heads_here = col_width // HD
    qkv_flat = w_qkv.reshape(w_qkv.shape[0], 3 * col_width)
    labels = tree_labels(seg_parent, token_depth)
    heads_seen = lax.axis_index("col") * heads_here + jnp.arange(heads_here, dtype=jnp.int32)
    slopes = jnp.exp2(-(heads_seen + 1).astype(jnp.float32))
    states = inputs.astype(jnp.float32)
    normed_one, inv_one, entry_one = normalize(states, ln1_gain, ln1_bias, feature_count)
    projected, entry_one_all = across_rows(entry_one, qkv_flat, False)
    tok_rows = projected.shape[0]
    projected = projected.reshape(tok_rows, 3, col_width)
    queries = (projected[:, 0] + b_qv[0]).astype(jnp.bfloat16)
    keys_here = projected[:, 1].astype(jnp.bfloat16)
    values_here = (projected[:, 2] + b_qv[1]).astype(jnp.bfloat16)
    pair_all = lax.all_gather(
        jnp.stack([keys_here, values_here], axis=1), "row", axis=0, tiled=True
    )
    key_rows = pair_all[:, 0].reshape(-1, heads_here, HD)
    value_rows = pair_all[:, 1].reshape(-1, heads_here, HD)
    query_heads = queries.reshape(tok_rows, heads_here, HD)
    offset = lax.axis_index("row") * tok_rows
    mixed, log_total = attention_forward(query_heads, key_rows, value_rows, labels, slopes, offset)
    mixed = mixed.reshape(tok_rows, col_width).astype(jnp.bfloat16)
    attn_out, mixed_all = across_cols(mixed, w_out, False)
    middle = states + attn_out + b_out
    normed_two, inv_two, entry_two = normalize(middle, ln2_gain, ln2_bias, feature_count)
    hidden_pre, entry_two_all = across_rows(entry_two, w_up, False)
    hidden_pre = hidden_pre + b_up
    hidden = gelu_value(hidden_pre).astype(jnp.bfloat16)
    ffn_out, hidden_all = across_cols(hidden, w_down, False)
    result = middle + ffn_out + b_down
    grad_hidden, down_all = across_rows(cotangent, w_down, True)
    grad_pre = (grad_hidden * gelu_slope(hidden_pre)).astype(jnp.bfloat16)
    grad_entry_two, pre_all = across_cols(grad_pre, w_up, True)
    grad_middle = cotangent.astype(jnp.float32) + normalize_back(
        grad_entry_two, normed_two, inv_two, ln2_gain, feature_count
    )
    grad_branch = grad_middle.astype(jnp.bfloat16)
    grad_mixed, branch_all = across_rows(grad_branch, w_out, True)
    grad_mixed = grad_mixed.astype(jnp.bfloat16).reshape(tok_rows, heads_here, HD)
    key_grad, value_grad, query_grad = attention_backward(
        query_heads, key_rows, value_rows, grad_mixed, log_total, labels, slopes, offset
    )
    kv_grads = lax.psum_scatter(
        jnp.stack([key_grad.reshape(-1, col_width), value_grad.reshape(-1, col_width)], axis=1),
        "row",
        scatter_dimension=0,
        tiled=True,
    )
    grad_projected = jnp.stack(
        [
            query_grad.reshape(tok_rows, col_width).astype(jnp.bfloat16),
            kv_grads[:, 0].astype(jnp.bfloat16),
            kv_grads[:, 1].astype(jnp.bfloat16),
        ],
        axis=1,
    )
    grad_entry_one, proj_all = across_cols(
        grad_projected.reshape(tok_rows, 3 * col_width), qkv_flat, True
    )
    input_grad = grad_middle + normalize_back(
        grad_entry_one, normed_one, inv_one, ln1_gain, feature_count
    )
    proj_sums = jnp.sum(proj_all.astype(jnp.float32), axis=0).reshape(3, col_width)
    weight_terms = (
        outer_sum(entry_one_all, proj_all).reshape(w_qkv.shape),
        jnp.stack([proj_sums[0], proj_sums[2]], axis=0),
        outer_sum(mixed_all, branch_all),
        jnp.sum(branch_all.astype(jnp.float32), axis=0),
        outer_sum(entry_two_all, pre_all),
        jnp.sum(pre_all.astype(jnp.float32), axis=0),
        outer_sum(hidden_all, down_all),
        jnp.sum(down_all.astype(jnp.float32), axis=0),
    )
    (
        grad_w_qkv,
        grad_b_qv,
        grad_w_out,
        grad_b_out,
        grad_w_up,
        grad_b_up,
        grad_w_down,
        grad_b_down,
    ) = lax.psum(
        (
            weight_terms[0],
            weight_terms[1],
            weight_terms[2],
            weight_terms[3],
            weight_terms[4],
            weight_terms[5],
            weight_terms[6],
            weight_terms[7],
        ),
        "dp",
    )
    norm_terms = (
        jnp.sum(grad_entry_one * normed_one, axis=0),
        jnp.sum(grad_entry_one, axis=0),
        jnp.sum(grad_entry_two * normed_two, axis=0),
        jnp.sum(grad_entry_two, axis=0),
    )
    grad_ln1_gain, grad_ln1_bias, grad_ln2_gain, grad_ln2_bias = lax.psum(
        (norm_terms[0], norm_terms[1], norm_terms[2], norm_terms[3]), ("dp", "col")
    )
    return (
        result,
        input_grad,
        grad_ln1_gain,
        grad_ln1_bias,
        grad_w_qkv,
        grad_b_qv,
        grad_w_out,
        grad_b_out,
        grad_ln2_gain,
        grad_ln2_bias,
        grad_w_up,
        grad_b_up,
        grad_w_down,
        grad_b_down,
    )


def solution(mesh):
    placed = (
        P(("dp", "col"), "row"),
        P(("dp", "col"), "row"),
        P("dp"),
        P("dp"),
        P("row"),
        P("row"),
        P("row", None, "col"),
        P(None, "col"),
        P("col", "row"),
        P("row"),
        P("row"),
        P("row"),
        P("row", "col"),
        P("col"),
        P("col", "row"),
        P("row"),
    )
    return jax.shard_map(
        on_device,
        mesh=mesh,
        in_specs=placed,
        out_specs=(
            P(("dp", "col"), "row"),
            P(("dp", "col"), "row"),
            P("row"),
            P("row"),
            P("row", None, "col"),
            P(None, "col"),
            P("col", "row"),
            P("row"),
            P("row"),
            P("row"),
            P("row", "col"),
            P("col"),
            P("col", "row"),
            P("row"),
        ),
        check_vma=False,
    )
```

profile of v0, /device:TPU:0, one launch (start us, length us, event | category | flops | bytes accessed | tf_op | source)
XLA Modules:
  0.0 1127.7 jit_solution(2528115706905828047)
XLA Ops:
  8.5 13.5 %all-reduce.4 = (f32[512]{0:T(512)S(1)}, f32[512]{0:T(512)S(1)}) all-reduce(f32[512]{0:T(512)S(1)} %get-tuple-element.134, f32[512]{0:T(512)S(1)} %get-tuple-element.133), channel_id=1, replica_groups=mesh['dp'=4,'row'=4,'col'=2] {'row'}, use_global_device_ids=true, to_apply=%region_3.4 | all-reduce | flops 1024 | bytes 8192 | tf_op jit(solution)/shard_map/psum | solution.py:23
  23.1 7.0 all_gather.27
  36.2 108.4 %reduce-scatter.10.cloned.1.call-done = f32[256,1536]{1,0:T(8,128)} async-done(((f32[1024,1536]{1,0:T(8,128)}), f32[256,1536]{1,0:T(8,128)}) %reduce-scatter.10.cloned.1.call-update) | async-done | bytes 1572880 | tf_op jit(solution)/shard_map/reduce_scatter | solution.py:64
  149.7 44.8 %all-gather.6.cloned.1.call-done = bf16[1024,2,512]{0,2,1:T(8,128)(2,1)} async-done(((bf16[256,2,512]{0,2,1:T(8,128)(2,1)}), bf16[1024,2,512]{0,2,1:T(8,128)(2,1)}) %all-gather.6.cloned.1.call-update) | async-done | bytes 2097168 | tf_op jit(solution)/shard_map/all_gather | solution.py:225
  201.1 28.5 %all-gather.8.cloned.1.call-done = bf16[1024,512]{0,1:T(8,128)(2,1)} async-done(((bf16[256,512]{0,1:T(8,128)(2,1)}), bf16[1024,512]{0,1:T(8,128)(2,1)}) %all-gather.8.cloned.1.call-update) | async-done | bytes 1048592 | tf_op jit(solution)/shard_map/all_gather | solution.py:75
  232.4 10.4 all_gather.32
  243.6 5.8 fusion.50
  253.7 10.6 all-reduce.3
  264.5 7.0 all_gather.30
  276.9 121.6 %reduce-scatter.18.cloned.1.call-done = f32[256,2048]{1,0:T(8,128)} async-done(((f32[1024,2048]{1,0:T(8,128)}), f32[256,2048]{1,0:T(8,128)}) %reduce-scatter.18.cloned.1.call-update) | async-done | bytes 2097168 | tf_op jit(solution)/shard_map/reduce_scatter | solution.py:64
  398.5 147.5 %reduce-scatter.14.cloned.1.call-done = f32[256,2048]{1,0:T(8,128)} async-done(((f32[1024,2048]{1,0:T(8,128)}), f32[256,2048]{1,0:T(8,128)}) %reduce-scatter.14.cloned.1.call-update) | async-done | bytes 2097168 | tf_op jit(solution)/shard_map/reduce_scatter | solution.py:64
  550.7 80.7 %all-gather.12.cloned.1.call-done = bf16[1024,2048]{1,0:T(8,128)(2,1)} async-done(((bf16[256,2048]{1,0:T(8,128)(2,1)}), bf16[1024,2048]{1,0:T(8,128)(2,1)}) %all-gather.12.cloned.1.call-update) | async-done | bytes 4194320 | tf_op jit(solution)/shard_map/all_gather | solution.py:75
  635.9 77.0 %all-gather.10.cloned.1.call-done = bf16[1024,2048]{1,0:T(8,128)(2,1)} async-done(((bf16[256,2048]{1,0:T(8,128)(2,1)}), bf16[1024,2048]{1,0:T(8,128)(2,1)}) %all-gather.10.cloned.1.call-update) | async-done | bytes 4194320 | tf_op jit(solution)/shard_map/all_gather | solution.py:75
  717.7 17.0 %reduce-scatter.20.cloned.1.call-done = f32[512,256]{1,0:T(8,128)} async-done(((f32[1024,256]{1,0:T(8,128)}), f32[512,256]{1,0:T(8,128)}) %reduce-scatter.20.cloned.1.call-update) | async-done | bytes 524304 | tf_op jit(solution)/shard_map/reduce_scatter | solution.py:82
  736.1 11.7 %all-reduce.2 = (f32[512]{0:T(512)S(1)}, f32[512]{0:T(512)S(1)}) all-reduce(f32[512]{0:T(512)S(1)} %get-tuple-element.124, f32[512]{0:T(512)S(1)} %get-tuple-element.128), channel_id=1, replica_groups=mesh['dp'=4,'row'=4,'col'=2] {'row'}, use_global_device_ids=true, to_apply=%region_21.22 | all-reduce | flops 1024 | bytes 8192 | tf_op jit(solution)/shard_map/psum | solution.py:23
  747.8 9.9 reduce-scatter.16.cloned.1.call-done
  760.1 8.7 all_gather.34
  770.7 44.0 %reduce-scatter.22.cloned.1.call-done = f32[256,512]{1,0:T(8,128)} async-done(((f32[1024,512]{1,0:T(8,128)}), f32[256,512]{1,0:T(8,128)}) %reduce-scatter.22.cloned.1.call-update) | async-done | bytes 524304 | tf_op jit(solution)/shard_map/reduce_scatter | solution.py:64
  827.4 73.4 %reduce-scatter.24.cloned.1.call-done = f32[256,2,512]{0,2,1:T(8,128)} async-done(((f32[1024,2,512]{0,2,1:T(8,128)}), f32[256,2,512]{0,2,1:T(8,128)}) %reduce-scatter.24.cloned.1.call-update) | async-done | bytes 1048592 | tf_op jit(solution)/shard_map/reduce_scatter | solution.py:254
  904.1 64.0 %all-gather.14.cloned.1.call-done = bf16[1024,1536]{0,1:T(8,128)(2,1)} async-done(((bf16[256,1536]{0,1:T(8,128)(2,1)}), bf16[1024,1536]{0,1:T(8,128)(2,1)}) %all-gather.14.cloned.1.call-update) | async-done | bytes 3145744 | tf_op jit(solution)/shard_map/all_gather | solution.py:75
  987.3 11.7 %all-reduce.5 = (f32[2,512]{1,0:T(2,128)}, f32[256]{0:T(256)}, f32[2048]{0:T(1024)}, f32[256]{0:T(256)}) all-reduce(f32[2,512]{1,0:T(2,128)S(1)} %pad_maximum_fusion.3, f32[256]{0:T(256)S(1)} %convert_reduce_fusion.3, f32[2048]{0:T(1024)S(1)} %convert_reduce_fusion, ...), channel_id=1, replica_groups=mesh['dp'=4,'row'=4,'col'=2] {'dp'}, use_global_device_ids=true, to_apply=%region_36.37 | all-reduce | flops 3584 | bytes 28672 | tf_op jit(solution)/shard_map/psum | solution.py:294
  1000.6 14.2 %all-reduce = (f32[256]{0:T(256)}, f32[256]{0:T(256)}, f32[256]{0:T(256)}, f32[256]{0:T(256)}) all-reduce(f32[256]{0:T(256)S(1)} %get-tuple-element.125, f32[256]{0:T(256)S(1)} %get-tuple-element.130, f32[256]{0:T(256)S(1)} %get-tuple-element.123, f32[256]{0:T(256)S(1)} %get-tuple-element.129), channel_id=1, replica_groups=mesh['dp'=4,'row'=4,'col'=2] {'dp','col'}, use_global_device_ids=true, to_apply=%region_31.32 | all-reduce | flops 1024 | bytes 8192 | tf_op jit(solution)/shard_map/psum | solution.py:313
  1014.8 8.9 all-reduce.1
  1025.9 88.7 %all-reduce.9.cloned.1.call-done = (f32[256,3,512]{0,2,1:T(8,128)}, f32[512,256]{1,0:T(8,128)}, f32[256,2048]{1,0:T(8,128)}, f32[2048,256]{1,0:T(8,128)}) async-done(((f32[256,3,512]{0,2,1:T(8,128)}, f32[512,256]{1,0:T(8,128)}, f32[256,2048]{1,0:T(8,128)}, f32[2048,256]{1,0:T(8,128)}), (f32[256,3,512]{0,2,1:T(8,128)}, f32[512,256]{1,0:T(8,128)}, f32[256,2048]{1,0:T(8,128)}, ...) | async-done | bytes 6291472 | tf_op jit(solution)/shard_map/psum | solution.py:294
  (171 shorter events, 98.3 us)
Async XLA Ops:
  7.2 265.1 %copy-start = (bf16[256,2048]{1,0:T(8,128)(2,1)S(1)}, bf16[256,2048]{1,0:T(8,128)(2,1)}, u32[]{:S(2)}) copy-start(bf16[256,2048]{1,0:T(8,128)(2,1)} %param.28) | copy-start | bytes 3145732
  7.2 137.4 %reduce-scatter.10.cloned.1.call-start = ((), (), s32[]{:S(2)}) async-start(), calls=%async_computation.9 | async-start | bytes 7864320 | tf_op jit(solution)/shard_map/reduce_scatter | solution.py:64
  35.5 159.0 %all-gather.6.cloned.1.call-start = ((), (), s32[]{:S(2)}) async-start(), calls=%async_computation.10 | async-start | bytes 2621440 | tf_op jit(solution)/shard_map/all_gather | solution.py:225
  36.2 111.5 %copy-start.26 = (s32[1024]{0:T(1024)S(1)}, s32[1024]{0:T(1024)}, u32[]{:S(2)}) copy-start(s32[1024]{0:T(1024)} %param.19) | copy-start | bytes 12292
  36.2 111.7 %copy-start.35 = (s32[13]{0:T(128)S(1)}, s32[13]{0:T(128)}, u32[]{:S(2)}) copy-start(s32[13]{0:T(128)} %param.18) | copy-start | bytes 160
  146.7 49.7 %copy-start.19 = (f32[256,1,512]{0,2,1:T(8,128)}, f32[256,1,512]{0,2,1:T(8,128)S(1)}, u32[]{:S(2)}) copy-start(f32[256,1,512]{0,2,1:T(8,128)S(1)} %get-tuple-element.162) | copy-start | bytes 1572868
  147.6 82.1 %all-gather.8.cloned.1.call-start = ((), (), s32[]{:S(2)}) async-start(), calls=%async_computation.11 | async-start | bytes 1310720 | tf_op jit(solution)/shard_map/all_gather | solution.py:75
  201.1 51.3 %reduce-scatter.12.cloned.1.call-start = ((), (), s32[]{:S(2)}) async-start(), calls=%async_computation.12 | async-start | bytes 1572864 | tf_op jit(solution)/shard_map/reduce_scatter | solution.py:82
  232.4 166.1 %reduce-scatter.18.cloned.1.call-start = ((), (), s32[]{:S(2)}) async-start(), calls=%async_computation.16 | async-start | bytes 10485760 | tf_op jit(solution)/shard_map/reduce_scatter | solution.py:64
  249.4 296.6 %reduce-scatter.14.cloned.1.call-start = ((), (), s32[]{:S(2)}) async-start(), calls=%async_computation.13 | async-start | bytes 10485760 | tf_op jit(solution)/shard_map/reduce_scatter | solution.py:64
  276.8 269.2 %copy-start.29 = (f32[2048]{0:T(1024)S(1)}, f32[2048]{0:T(1024)}, u32[]{:S(2)}) copy-start(f32[2048]{0:T(1024)} %param.29) | copy-start | bytes 24580
  276.8 354.5 %all-gather.12.cloned.1.call-start = ((), (), s32[]{:S(2)}) async-start(), calls=%async_computation.17 | async-start | bytes 5242880 | tf_op jit(solution)/shard_map/all_gather | solution.py:75
  549.7 163.2 %all-gather.10.cloned.1.call-start = ((), (), s32[]{:S(2)}) async-start(), calls=%async_computation.14 | async-start | bytes 5242880 | tf_op jit(solution)/shard_map/all_gather | solution.py:75
  550.5 184.2 %reduce-scatter.20.cloned.1.call-start = ((), (), s32[]{:S(2)}) async-start(), calls=%async_computation.18 | async-start | bytes 1572864 | tf_op jit(solution)/shard_map/reduce_scatter | solution.py:82
  635.8 121.9 %copy-start.32 = (f32[256]{0:T(256)S(1)}, f32[256]{0:T(256)}, u32[]{:S(2)}) copy-start(f32[256]{0:T(256)} %param.31) | copy-start | bytes 3076
  635.8 121.9 %reduce-scatter.16.cloned.1.call-start = ((), (), s32[]{:S(2)}) async-start(), calls=%async_computation.15 | async-start | bytes 1572864 | tf_op jit(solution)/shard_map/reduce_scatter | solution.py:82
  717.6 97.0 %reduce-scatter.22.cloned.1.call-start = ((), (), s32[]{:S(2)}) async-start(), calls=%async_computation.19 | async-start | bytes 2621440 | tf_op jit(solution)/shard_map/reduce_scatter | solution.py:64
  770.6 130.2 %reduce-scatter.24.cloned.1.call-start = ((), (), s32[]{:S(2)}) async-start(), calls=%async_computation.20 | async-start | bytes 5242880 | tf_op jit(solution)/shard_map/reduce_scatter | solution.py:254
  824.6 143.5 %all-gather.14.cloned.1.call-start = ((), (), s32[]{:S(2)}) async-start(), calls=%async_computation.21 | async-start | bytes 3932160 | tf_op jit(solution)/shard_map/all_gather | solution.py:75
  827.4 140.7 %copy-start.14 = (bf16[256,3,512]{0,2,1:T(8,128)(2,1)S(1)}, bf16[256,3,512]{0,2,1:T(8,128)(2,1)}, u32[]{:S(2)}) copy-start(bf16[256,3,512]{0,2,1:T(8,128)(2,1)} %copy-done.13) | copy-start | bytes 2359300
  904.0 68.3 %copy-start.16 = (bf16[1024,256]{1,0:T(8,128)(2,1)S(1)}, bf16[1024,256]{1,0:T(8,128)(2,1)}, u32[]{:S(2)}) copy-start(bf16[1024,256]{1,0:T(8,128)(2,1)} %copy-done.15) | copy-start | bytes 1572868
  904.0 95.0 %reduce-scatter.26.cloned.1.call-start = ((), (), s32[]{:S(2)}) async-start(), calls=%async_computation.22 | async-start | bytes 1572864 | tf_op jit(solution)/shard_map/reduce_scatter | solution.py:82
  972.0 142.6 %all-reduce.9.cloned.1.call-start = ((), (), s32[]{:S(2)}) async-start(), calls=%async_computation.23 | async-start | bytes 12582912 | tf_op jit(solution)/shard_map/psum | solution.py:294
  986.6 37.1 %copy-start.21 = (f32[512,256]{1,0:T(8,128)S(1)}, f32[512,256]{1,0:T(8,128)}, u32[]{:S(2)}) copy-start(f32[512,256]{1,0:T(8,128)} %get-tuple-element.156) | copy-start | bytes 1572868
  (27 other events, 171.5 us)
Sparse Core Ops, SparseCore 0:
  35.6 108.9 reduce-scatter.9
  147.7 46.7 all-gather.5
  201.2 28.4 all-gather.7
  232.5 19.8 reduce-scatter.11
  254.7 143.6 reduce-scatter.17
  400.8 145.1 reduce-scatter.13
  549.8 81.4 all-gather.11
  633.6 79.2 all-gather.9
  715.8 18.8 reduce-scatter.19
  737.3 20.3 reduce-scatter.15
  770.7 43.8 reduce-scatter.21
  824.7 76.0 reduce-scatter.23
  904.1 63.9 all-gather.13
  972.2 18.4 reduce-scatter.25
  994.3 120.2 all-reduce.8
where the time goes:
time: 1130 us
  waiting for transfers between devices  909 us (80%)
  blocking collectives  104 us (9%)
  matrix products  53.8 us (5%)
  other arithmetic  30.3 us (3%)
  local copies, waits for them, and re-layouts  15.1 us (1%)
  between operations  14.3 us (1%)
    reduce_scatter x4, waiting for transfers between devices, across_rows(): lax.psum_scatter(partial_term(jnp.int32(0), row_count * lax.axis_size('ro...  422 us
    all_gather x4, waiting for transfers between devices, across_cols(): gathered = lax.all_gather(operand, 'row', axis=0, tiled=True)  250 us
    psum x1, waiting for transfers between devices, on_device(): lax.psum((weight_terms[0], weight_terms[1], weight_terms[2], weight_terms...  88.7 us
    reduce_scatter x1, waiting for transfers between devices, on_device(): lax.psum_scatter(jnp.stack([key_grad.reshape(-1, col_width), value_grad.r...  73.4 us
    all_gather x1, waiting for transfers between devices, on_device(): lax.all_gather(jnp.stack([keys_here, values_here], axis=1), 'row', axis=0...  44.8 us
    psum x4, blocking collectives, width_sums(): lax.psum((jnp.sum(first_term, axis=1), jnp.sum(second_term, axis=1)), 'row')  44.6 us
    all_gather x4, blocking collectives, across_rows(): gathered = lax.all_gather(operand, 'col', axis=0, tiled=True)  33.2 us
    reduce_scatter x4, waiting for transfers between devices, across_cols(): lax.psum_scatter(partial_term(jnp.int32(0), row_count * lax.axis_size('co...  29.8 us
  transfers between devices with their start and end apart: 15, of which 14 were waited for; matrix products, arithmetic and copies ran while one was open for 4% of the time, Pallas kernels for 0%

commit v1 on v0

--- a/solution.py
+++ b/solution.py
@@ -222,9 +222,13 @@
     queries = (projected[:, 0] + b_qv[0]).astype(jnp.bfloat16)
     keys_here = projected[:, 1].astype(jnp.bfloat16)
     values_here = (projected[:, 2] + b_qv[1]).astype(jnp.bfloat16)
-    pair_all = lax.all_gather(
-        jnp.stack([keys_here, values_here], axis=1), "row", axis=0, tiled=True
-    )
+    x = jnp.stack([keys_here, values_here], axis=1)
+    ways, here, step = (lax.axis_size("row"), lax.axis_index("row"), x.shape[0])
+    lengths = [n * ways if d == 0 else n for d, n in enumerate(x.shape)]
+    pair_all = lax.dynamic_update_slice_in_dim(jnp.zeros(lengths, x.dtype), x, here * step, axis=0)
+    for far in range(1, ways):
+        x = lax.ppermute(x, "row", [(d, (d + 1) % ways) for d in range(ways)])
+        pair_all = lax.dynamic_update_slice_in_dim(pair_all, x, (here - far) % ways * step, axis=0)
     key_rows = pair_all[:, 0].reshape(-1, heads_here, HD)
     value_rows = pair_all[:, 1].reshape(-1, heads_here, HD)
     query_heads = queries.reshape(tok_rows, heads_here, HD)

time: 1130 us -> 1130 us (level)
    all_gather x1 -> x0, waiting for transfers between devices: 44.8 us -> none  [on_device(): lax.all_gather(jnp.stack([keys_here, values_here], axis=1), 'row', axis=0...]
    ppermute x0 -> x3, waiting for transfers between devices: none -> 39.9 us  [on_device(): x = lax.ppermute(x, 'row', [(d, (d + 1) % ways) for d in range(ways)])]
  transfers between devices with their start and end apart: 15 -> 17, of which waited for: 14 -> 16; matrix products, arithmetic and copies ran while one was open for 4% -> 4% of each run, Pallas kernels for 0% -> 0%
where the time goes in v1:
time: 1130 us
  waiting for transfers between devices  906 us (80%)
  blocking collectives  104 us (9%)
  matrix products  52.3 us (5%)
  other arithmetic  30.1 us (3%)
  local copies, waits for them, and re-layouts  17.3 us (2%)
  between operations  14.4 us (1%)
    reduce_scatter x4, waiting for transfers between devices, across_rows(): lax.psum_scatter(partial_term(jnp.int32(0), row_count * lax.axis_size('ro...  421 us
    all_gather x4, waiting for transfers between devices, across_cols(): gathered = lax.all_gather(operand, 'row', axis=0, tiled=True)  250 us
    psum x1, waiting for transfers between devices, on_device(): lax.psum((weight_terms[0], weight_terms[1], weight_terms[2], weight_terms...  88.7 us
    reduce_scatter x1, waiting for transfers between devices, on_device(): lax.psum_scatter(jnp.stack([key_grad.reshape(-1, col_width), value_grad.r...  73.4 us
    psum x4, blocking collectives, width_sums(): lax.psum((jnp.sum(first_term, axis=1), jnp.sum(second_term, axis=1)), 'row')  44.6 us
    ppermute x3, waiting for transfers between devices, on_device(): x = lax.ppermute(x, 'row', [(d, (d + 1) % ways) for d in range(ways)])  39.9 us
    all_gather x4, blocking collectives, across_rows(): gathered = lax.all_gather(operand, 'col', axis=0, tiled=True)  33.2 us
    reduce_scatter x4, waiting for transfers between devices, across_cols(): lax.psum_scatter(partial_term(jnp.int32(0), row_count * lax.axis_size('co...  31.5 us
  transfers between devices with their start and end apart: 17, of which 16 were waited for; matrix products, arithmetic and copies ran while one was open for 4% of the time, Pallas kernels for 0%

profile of v1, /device:TPU:0, one launch (start us, length us, event | category | flops | bytes accessed | tf_op | source)
XLA Modules:
  0.0 1126.6 jit_solution(4954430919635949657)
XLA Ops:
  8.5 13.5 %all-reduce.4 = (f32[512]{0:T(512)S(1)}, f32[512]{0:T(512)S(1)}) all-reduce(f32[512]{0:T(512)S(1)} %get-tuple-element.134, f32[512]{0:T(512)S(1)} %get-tuple-element.133), channel_id=1, replica_groups=mesh['dp'=4,'row'=4,'col'=2] {'row'}, use_global_device_ids=true, to_apply=%region_3.4 | all-reduce | flops 1024 | bytes 8192 | tf_op jit(solution)/shard_map/psum | solution.py:23
  23.1 7.0 all_gather.24
  36.2 108.4 %reduce-scatter.10.cloned.1.call-done = f32[256,1536]{1,0:T(8,128)} async-done(((f32[1024,1536]{1,0:T(8,128)}), f32[256,1536]{1,0:T(8,128)}) %reduce-scatter.10.cloned.1.call-update) | async-done | bytes 1572880 | tf_op jit(solution)/shard_map/reduce_scatter | solution.py:64
  150.2 14.3 %collective-permute-done = bf16[256,2,512]{0,2,1:T(8,128)(2,1)} collective-permute-done((bf16[256,2,512]{0,2,1:T(8,128)(2,1)}, bf16[256,2,512]{0,2,1:T(8,128)(2,1)}, u32[]{:S(2)}, u32[]{:S(2)}) %collective-permute-start) | collective-permute-done | bytes 524320 | tf_op jit(solution)/shard_map/ppermute | solution.py:230
  165.3 14.2 %collective-permute-done.1 = bf16[256,2,512]{0,2,1:T(8,128)(2,1)} collective-permute-done((bf16[256,2,512]{0,2,1:T(8,128)(2,1)}, bf16[256,2,512]{0,2,1:T(8,128)(2,1)}, u32[]{:S(2)}, u32[]{:S(2)}) %collective-permute-start.1) | collective-permute-done | bytes 524320 | tf_op jit(solution)/shard_map/ppermute | solution.py:230
  181.9 11.5 %collective-permute-done.2 = bf16[256,2,512]{0,2,1:T(8,128)(2,1)} collective-permute-done((bf16[256,2,512]{0,2,1:T(8,128)(2,1)}, bf16[256,2,512]{0,2,1:T(8,128)(2,1)}, u32[]{:S(2)}, u32[]{:S(2)}) %collective-permute-start.2) | collective-permute-done | bytes 524320 | tf_op jit(solution)/shard_map/ppermute | solution.py:230
  199.6 28.5 %all-gather.5.cloned.1.call-done = bf16[1024,512]{0,1:T(8,128)(2,1)} async-done(((bf16[256,512]{0,1:T(8,128)(2,1)}), bf16[1024,512]{0,1:T(8,128)(2,1)}) %all-gather.5.cloned.1.call-update) | async-done | bytes 1048592 | tf_op jit(solution)/shard_map/all_gather | solution.py:75
  230.8 10.4 all_gather.28
  252.0 10.6 all-reduce.3
  275.4 121.4 %reduce-scatter.18.cloned.1.call-done = f32[256,2048]{1,0:T(8,128)} async-done(((f32[1024,2048]{1,0:T(8,128)}), f32[256,2048]{1,0:T(8,128)}) %reduce-scatter.18.cloned.1.call-update) | async-done | bytes 2097168 | tf_op jit(solution)/shard_map/reduce_scatter | solution.py:64
  396.8 147.5 %reduce-scatter.14.cloned.1.call-done = f32[256,2048]{1,0:T(8,128)} async-done(((f32[1024,2048]{1,0:T(8,128)}), f32[256,2048]{1,0:T(8,128)}) %reduce-scatter.14.cloned.1.call-update) | async-done | bytes 2097168 | tf_op jit(solution)/shard_map/reduce_scatter | solution.py:64
  548.9 80.8 %all-gather.9.cloned.1.call-done = bf16[1024,2048]{1,0:T(8,128)(2,1)} async-done(((bf16[256,2048]{1,0:T(8,128)(2,1)}), bf16[1024,2048]{1,0:T(8,128)(2,1)}) %all-gather.9.cloned.1.call-update) | async-done | bytes 4194320 | tf_op jit(solution)/shard_map/all_gather | solution.py:75
  634.2 77.0 %all-gather.7.cloned.1.call-done = bf16[1024,2048]{1,0:T(8,128)(2,1)} async-done(((bf16[256,2048]{1,0:T(8,128)(2,1)}), bf16[1024,2048]{1,0:T(8,128)(2,1)}) %all-gather.7.cloned.1.call-update) | async-done | bytes 4194320 | tf_op jit(solution)/shard_map/all_gather | solution.py:75
  715.7 17.3 %reduce-scatter.20.cloned.1.call-done = f32[512,256]{1,0:T(8,128)} async-done(((f32[1024,256]{1,0:T(8,128)}), f32[512,256]{1,0:T(8,128)}) %reduce-scatter.20.cloned.1.call-update) | async-done | bytes 524304 | tf_op jit(solution)/shard_map/reduce_scatter | solution.py:82
  734.4 11.7 %all-reduce.2 = (f32[512]{0:T(512)S(1)}, f32[512]{0:T(512)S(1)}) all-reduce(f32[512]{0:T(512)S(1)} %get-tuple-element.124, f32[512]{0:T(512)S(1)} %get-tuple-element.128), channel_id=1, replica_groups=mesh['dp'=4,'row'=4,'col'=2] {'row'}, use_global_device_ids=true, to_apply=%region_21.22 | all-reduce | flops 1024 | bytes 8192 | tf_op jit(solution)/shard_map/psum | solution.py:23
  746.1 10.1 reduce-scatter.16.cloned.1.call-done
  758.6 8.7 all_gather.30
  769.2 44.0 %reduce-scatter.22.cloned.1.call-done = f32[256,512]{1,0:T(8,128)} async-done(((f32[1024,512]{1,0:T(8,128)}), f32[256,512]{1,0:T(8,128)}) %reduce-scatter.22.cloned.1.call-update) | async-done | bytes 524304 | tf_op jit(solution)/shard_map/reduce_scatter | solution.py:64
  826.2 73.4 %reduce-scatter.24.cloned.1.call-done = f32[256,2,512]{0,2,1:T(8,128)} async-done(((f32[1024,2,512]{0,2,1:T(8,128)}), f32[256,2,512]{0,2,1:T(8,128)}) %reduce-scatter.24.cloned.1.call-update) | async-done | bytes 1048592 | tf_op jit(solution)/shard_map/reduce_scatter | solution.py:258
  902.9 64.0 %all-gather.11.cloned.1.call-done = bf16[1024,1536]{0,1:T(8,128)(2,1)} async-done(((bf16[256,1536]{0,1:T(8,128)(2,1)}), bf16[1024,1536]{0,1:T(8,128)(2,1)}) %all-gather.11.cloned.1.call-update) | async-done | bytes 3145744 | tf_op jit(solution)/shard_map/all_gather | solution.py:75
  986.1 11.7 %all-reduce.5 = (f32[2,512]{1,0:T(2,128)}, f32[256]{0:T(256)}, f32[2048]{0:T(1024)}, f32[256]{0:T(256)}) all-reduce(f32[2,512]{1,0:T(2,128)S(1)} %pad_maximum_fusion.3, f32[256]{0:T(256)S(1)} %convert_reduce_fusion.3, f32[2048]{0:T(1024)S(1)} %convert_reduce_fusion, ...), channel_id=1, replica_groups=mesh['dp'=4,'row'=4,'col'=2] {'dp'}, use_global_device_ids=true, to_apply=%region_36.37 | all-reduce | flops 3584 | bytes 28672 | tf_op jit(solution)/shard_map/psum | solution.py:298
  999.4 14.2 %all-reduce = (f32[256]{0:T(256)}, f32[256]{0:T(256)}, f32[256]{0:T(256)}, f32[256]{0:T(256)}) all-reduce(f32[256]{0:T(256)S(1)} %get-tuple-element.125, f32[256]{0:T(256)S(1)} %get-tuple-element.130, f32[256]{0:T(256)S(1)} %get-tuple-element.123, f32[256]{0:T(256)S(1)} %get-tuple-element.129), channel_id=1, replica_groups=mesh['dp'=4,'row'=4,'col'=2] {'dp','col'}, use_global_device_ids=true, to_apply=%region_31.32 | all-reduce | flops 1024 | bytes 8192 | tf_op jit(solution)/shard_map/psum | solution.py:317
  1013.6 8.9 all-reduce.1
  1024.7 88.7 %all-reduce.9.cloned.1.call-done = (f32[256,3,512]{0,2,1:T(8,128)}, f32[512,256]{1,0:T(8,128)}, f32[256,2048]{1,0:T(8,128)}, f32[2048,256]{1,0:T(8,128)}) async-done(((f32[256,3,512]{0,2,1:T(8,128)}, f32[512,256]{1,0:T(8,128)}, f32[256,2048]{1,0:T(8,128)}, f32[2048,256]{1,0:T(8,128)}), (f32[256,3,512]{0,2,1:T(8,128)}, f32[512,256]{1,0:T(8,128)}, f32[256,2048]{1,0:T(8,128)}, ...) | async-done | bytes 6291472 | tf_op jit(solution)/shard_map/psum | solution.py:298
  (182 shorter events, 114.3 us)
Async XLA Ops:
  7.2 263.5 %copy-start = (bf16[256,2048]{1,0:T(8,128)(2,1)S(1)}, bf16[256,2048]{1,0:T(8,128)(2,1)}, u32[]{:S(2)}) copy-start(bf16[256,2048]{1,0:T(8,128)(2,1)} %param.28) | copy-start | bytes 3145732
  7.2 137.4 %reduce-scatter.10.cloned.1.call-start = ((), (), s32[]{:S(2)}) async-start(), calls=%async_computation.9 | async-start | bytes 7864320 | tf_op jit(solution)/shard_map/reduce_scatter | solution.py:64
  35.5 192.5 %all-gather.5.cloned.1.call-start = ((), (), s32[]{:S(2)}) async-start(), calls=%async_computation.10 | async-start | bytes 1310720 | tf_op jit(solution)/shard_map/all_gather | solution.py:75
  148.6 15.8 %collective-permute-start = (bf16[256,2,512]{0,2,1:T(8,128)(2,1)}, bf16[256,2,512]{0,2,1:T(8,128)(2,1)}, u32[]{:S(2)}, u32[]{:S(2)}) collective-permute-start(bf16[256,2,512]{0,2,1:T(8,128)(2,1)} %get-tuple-element.165), channel_id=1, source_target_pairs={{0,2},{2,4},{4,6},{6,0},{1,3},{3,5},{5,7},{7,1},{8,10},{10,12},{12... | collective-permute-start | bytes 1572872 | tf_op jit(solution)/shard_map/ppermute | solution.py:230
  164.4 15.0 %collective-permute-start.1 = (bf16[256,2,512]{0,2,1:T(8,128)(2,1)}, bf16[256,2,512]{0,2,1:T(8,128)(2,1)}, u32[]{:S(2)}, u32[]{:S(2)}) collective-permute-start(bf16[256,2,512]{0,2,1:T(8,128)(2,1)} %collective-permute-done), channel_id=1, source_target_pairs={{0,2},{2,4},{4,6},{6,0},{1,3},{3,5},{5,7},{7,1},{8,10},{10,12},{12... | collective-permute-start | bytes 1572872 | tf_op jit(solution)/shard_map/ppermute | solution.py:230
  179.4 14.1 %collective-permute-start.2 = (bf16[256,2,512]{0,2,1:T(8,128)(2,1)}, bf16[256,2,512]{0,2,1:T(8,128)(2,1)}, u32[]{:S(2)}, u32[]{:S(2)}) collective-permute-start(bf16[256,2,512]{0,2,1:T(8,128)(2,1)} %collective-permute-done.1), channel_id=1, source_target_pairs={{0,2},{2,4},{4,6},{6,0},{1,3},{3,5},{5,7},{7,1},{8,10},{10,12},{12... | collective-permute-start | bytes 1572872 | tf_op jit(solution)/shard_map/ppermute | solution.py:230
  199.5 42.5 %copy-start.24 = (bf16[2048,256]{1,0:T(8,128)(2,1)S(1)}, bf16[2048,256]{1,0:T(8,128)(2,1)}, u32[]{:S(2)}) copy-start(bf16[2048,256]{1,0:T(8,128)(2,1)} %param.30) | copy-start | bytes 3145732
  199.5 51.3 %reduce-scatter.12.cloned.1.call-start = ((), (), s32[]{:S(2)}) async-start(), calls=%async_computation.11 | async-start | bytes 1572864 | tf_op jit(solution)/shard_map/reduce_scatter | solution.py:82
  230.7 166.1 %reduce-scatter.18.cloned.1.call-start = ((), (), s32[]{:S(2)}) async-start(), calls=%async_computation.15 | async-start | bytes 10485760 | tf_op jit(solution)/shard_map/reduce_scatter | solution.py:64
  246.5 297.8 %reduce-scatter.14.cloned.1.call-start = ((), (), s32[]{:S(2)}) async-start(), calls=%async_computation.12 | async-start | bytes 10485760 | tf_op jit(solution)/shard_map/reduce_scatter | solution.py:64
  275.2 269.2 %copy-start.31 = (f32[2048]{0:T(1024)S(1)}, f32[2048]{0:T(1024)}, u32[]{:S(2)}) copy-start(f32[2048]{0:T(1024)} %param.29) | copy-start | bytes 24580
  275.2 354.5 %all-gather.9.cloned.1.call-start = ((), (), s32[]{:S(2)}) async-start(), calls=%async_computation.16 | async-start | bytes 5242880 | tf_op jit(solution)/shard_map/all_gather | solution.py:75
  548.1 163.2 %all-gather.7.cloned.1.call-start = ((), (), s32[]{:S(2)}) async-start(), calls=%async_computation.13 | async-start | bytes 5242880 | tf_op jit(solution)/shard_map/all_gather | solution.py:75
  548.8 184.2 %reduce-scatter.20.cloned.1.call-start = ((), (), s32[]{:S(2)}) async-start(), calls=%async_computation.17 | async-start | bytes 1572864 | tf_op jit(solution)/shard_map/reduce_scatter | solution.py:82
  634.2 122.0 %copy-start.34 = (f32[256]{0:T(256)S(1)}, f32[256]{0:T(256)}, u32[]{:S(2)}) copy-start(f32[256]{0:T(256)} %param.31) | copy-start | bytes 3076
  634.2 122.0 %reduce-scatter.16.cloned.1.call-start = ((), (), s32[]{:S(2)}) async-start(), calls=%async_computation.14 | async-start | bytes 1572864 | tf_op jit(solution)/shard_map/reduce_scatter | solution.py:82
  715.7 97.4 %reduce-scatter.22.cloned.1.call-start = ((), (), s32[]{:S(2)}) async-start(), calls=%async_computation.18 | async-start | bytes 2621440 | tf_op jit(solution)/shard_map/reduce_scatter | solution.py:64
  769.1 130.5 %reduce-scatter.24.cloned.1.call-start = ((), (), s32[]{:S(2)}) async-start(), calls=%async_computation.19 | async-start | bytes 5242880 | tf_op jit(solution)/shard_map/reduce_scatter | solution.py:258
  823.4 143.5 %all-gather.11.cloned.1.call-start = ((), (), s32[]{:S(2)}) async-start(), calls=%async_computation.20 | async-start | bytes 3932160 | tf_op jit(solution)/shard_map/all_gather | solution.py:75
  826.2 140.7 %copy-start.16 = (bf16[256,3,512]{0,2,1:T(8,128)(2,1)S(1)}, bf16[256,3,512]{0,2,1:T(8,128)(2,1)}, u32[]{:S(2)}) copy-start(bf16[256,3,512]{0,2,1:T(8,128)(2,1)} %copy-done.15) | copy-start | bytes 2359300
  902.8 68.3 %copy-start.18 = (bf16[1024,256]{1,0:T(8,128)(2,1)S(1)}, bf16[1024,256]{1,0:T(8,128)(2,1)}, u32[]{:S(2)}) copy-start(bf16[1024,256]{1,0:T(8,128)(2,1)} %copy-done.17) | copy-start | bytes 1572868
  902.9 94.9 %reduce-scatter.26.cloned.1.call-start = ((), (), s32[]{:S(2)}) async-start(), calls=%async_computation.21 | async-start | bytes 1572864 | tf_op jit(solution)/shard_map/reduce_scatter | solution.py:82
  970.9 142.6 %all-reduce.9.cloned.1.call-start = ((), (), s32[]{:S(2)}) async-start(), calls=%async_computation.22 | async-start | bytes 12582912 | tf_op jit(solution)/shard_map/psum | solution.py:298
  985.4 37.1 %copy-start.23 = (f32[512,256]{1,0:T(8,128)S(1)}, f32[512,256]{1,0:T(8,128)}, u32[]{:S(2)}) copy-start(f32[512,256]{1,0:T(8,128)} %get-tuple-element.156) | copy-start | bytes 1572868
  (31 other events, 202.3 us)
Sparse Core Ops, SparseCore 0:
  35.6 108.9 reduce-scatter.9
  199.6 28.3 all-gather.4
  230.8 19.8 reduce-scatter.11
  253.1 143.6 reduce-scatter.17
  399.1 145.1 reduce-scatter.13
  548.2 81.4 all-gather.8
  631.9 79.2 all-gather.6
  714.1 18.8 reduce-scatter.19
  735.8 20.3 reduce-scatter.15
  769.2 43.8 reduce-scatter.21
  823.5 76.0 reduce-scatter.23
  903.0 63.9 all-gather.10
  971.0 18.4 reduce-scatter.25
  993.1 120.2 all-reduce.8
